TPU v7x, 512 devices: a whole 4x4x16 slice. The times are simulated.
512 devices in a mesh: slab: 128 (over y, z, core), sub: 4 (over x).
Axes of the slice: x: 4, y: 4, z: 16, core: 2. Of those that a mesh axis runs over, the one named last changes fastest.
Arguments:
- mode_shapes: bfloat16 [32, 6, 1024, 512], P(None, None, 'slab', 'sub')
- span_stiff: float32 [6, 1024, 512], P(None, 'slab', 'sub'), may hold values from -4 to 4
- chord_stiff: float32 [6, 1024, 512], P(None, 'slab', 'sub'), may hold values from -4 to 4
- span_geo: float32 [1024, 512], P('slab', 'sub'), may hold values from 0.2 to 2
- chord_geo: float32 [1024, 512], P('slab', 'sub'), may hold values from 0.2 to 2
- ground: float32 [6, 1024, 512], P(None, 'slab', 'sub'), may hold values from 0.2 to 2
- chord_len: int32 [1024], replicated, may hold values from 192 to 512, as said below
Outputs:
- adjoint: float32 [32, 6, 1024, 512], P(None, None, 'slab', 'sub')
- residual: float32 [32, 6, 1024, 512], P(None, None, 'slab', 'sub')
Inputs may be any that keep to these rules, and one draw needn't show every extreme that they name: chord_len[0] = 512.
All inputs are finite; a program needn't handle non-finite values.
Results may differ from a plain program's by a relative error of at most 0.0003.
Values sent between devices are 32-bit elements; how exact they have to be, the bound alone decides.
A program may use at most 64 MiB of HBM per device.

v0:
```python
import jax
import jax.numpy as jnp
from jax import lax
from jax.sharding import PartitionSpec as P

ITERS = 2


def from_behind(value, axis, steps):
    count = lax.axis_size(axis)
    initial, last = (max(0, -steps), min(count, count - steps))
    return lax.ppermute(value, axis, [(source, source + steps) for source in range(initial, last)])


def factor_blocks(blocks):
    count = len(blocks)
    factor = [[None] * count for i in range(count)]
    inverse = [None] * count
    for j in range(count):
        running = blocks[j][j]
        for k in range(j):
            running = running - factor[j][k] * factor[j][k]
        diag_root = jnp.sqrt(running)
        factor[j][j] = diag_root
        inverse[j] = 1.0 / diag_root
        for i in range(j + 1, count):
            running = blocks[i][j]
            for k in range(j):
                running = running - factor[i][k] * factor[j][k]
            factor[i][j] = running * inverse[j]
    return (factor, inverse)


def solve_blocks(factor, inverse, vector):
    count = len(inverse)
    forward = []
    for i in range(count):
        running = vector[:, i]
        for j in range(i):
            running = running - factor[i][j][None] * forward[j]
        forward.append(running * inverse[i][None])
    backward = [None] * count
    for i in reversed(range(count)):
        running = forward[i]
        for j in range(i + 1, count):
            running = running - factor[j][i][None] * backward[j]
        backward[i] = running * inverse[i][None]
    return jnp.stack(backward, axis=1)


def neighbours_ahead(field):
    next_station = from_behind(field[:, :, :1, :], "slab", -1)
    next_column = from_behind(field[:, :, :, :1], "sub", -1)
    span_next = jnp.concatenate([field[:, :, 1:, :], next_station], axis=2)
    chord_next = jnp.concatenate([field[:, :, :, 1:], next_column], axis=3)
    return (span_next, chord_next)


def forces_behind(span_forces, chord_forces):
    from_span = from_behind(span_forces[:, :, -1:, :], "slab", 1)
    from_chord = from_behind(chord_forces[:, :, :, -1:], "sub", 1)
    span_part = jnp.concatenate([from_span, span_forces[:, :, :-1, :]], axis=2)
    chord_part = jnp.concatenate([from_chord, chord_forces[:, :, :, :-1]], axis=3)
    return span_part + chord_part


def edge_forces(stiffness, jump, live_mask):
    strain = jnp.sum(stiffness[None] * jump, axis=1) * live_mask[None]
    return stiffness[None] * strain[:, None]


def operate_sent(field, span_stiff, chord_stiff, span_live, chord_live, ground):
    span_next, chord_next = neighbours_ahead(field)
    span_forces = edge_forces(span_stiff, span_next - field, span_live)
    chord_forces = edge_forces(chord_stiff, chord_next - field, chord_live)
    return (
        ground[None] * field - span_forces - chord_forces + forces_behind(span_forces, chord_forces)
    )


def inner_rz(first, second):
    return lax.psum(jnp.sum(first * second, axis=(1, 2, 3)), ("slab", "sub"))


def inner_pq(first, second):
    return lax.psum(jnp.sum(first * second, axis=(1, 2, 3)), ("slab", "sub"))


def body(mode_shapes, span_stiff, chord_stiff, span_geo, chord_geo, ground, chord_len):
    count = ground.shape[0]
    stations = ground.shape[1]
    columns = ground.shape[2]
    row_start = lax.axis_index("slab") * stations
    col_start = lax.axis_index("sub") * columns
    padded_len = jnp.concatenate(
        [jnp.zeros((1,), jnp.int32), chord_len, jnp.zeros((2,), jnp.int32)]
    )
    window = lax.dynamic_slice_in_dim(padded_len, row_start, stations + 2)
    col_global = (col_start + jnp.arange(columns, dtype=jnp.int32))[None, :]
    span_mask_wide = ((col_global < window[:-1, None]) & (col_global < window[1:, None])).astype(
        jnp.float32
    )
    col_wide = (col_start - 1 + jnp.arange(columns + 1, dtype=jnp.int32))[None, :]
    own_len = window[1 : stations + 1, None]
    chord_mask_wide = ((col_wide + 1 < own_len) & (col_wide >= 0)).astype(jnp.float32)
    span_live = span_mask_wide[1:]
    chord_live = chord_mask_wide[:, 1:]
    ghost_span = from_behind(span_stiff[:, stations - 1 :, :], "slab", 1)
    ghost_chord = from_behind(chord_stiff[:, :, columns - 1 :], "sub", 1)
    span_wide = jnp.concatenate([ghost_span, span_stiff], axis=1)
    chord_wide = jnp.concatenate([ghost_chord, chord_stiff], axis=2)
    blocks = []
    for i in range(count):
        block_row = []
        for j in range(count):
            span_pair = span_wide[i] * span_wide[j] * span_mask_wide
            chord_pair = chord_wide[i] * chord_wide[j] * chord_mask_wide
            entry = span_pair[1:] + span_pair[:-1] + chord_pair[:, 1:] + chord_pair[:, :-1]
            if i == j:
                entry = entry + ground[i]
            block_row.append(entry)
        blocks.append(block_row)
    factor, inverse = factor_blocks(blocks)
    mode_field = mode_shapes.astype(jnp.float32)
    span_next, chord_next = neighbours_ahead(mode_field)
    span_jump = span_next - mode_field
    chord_jump = chord_next - mode_field
    span_weight = jnp.sum(span_jump * span_jump, axis=1) * (span_geo * span_live)[None]
    chord_weight = jnp.sum(chord_jump * chord_jump, axis=1) * (chord_geo * chord_live)[None]
    span_load = span_stiff[None] * span_weight[:, None]
    chord_load = chord_stiff[None] * chord_weight[:, None]
    load = forces_behind(span_load, chord_load) - span_load - chord_load
    solution = jnp.zeros_like(load)
    residual = load
    precond = solve_blocks(factor, inverse, residual)
    direction = precond
    precond_norm = inner_rz(residual, precond)
    for step in range(ITERS):
        image = operate_sent(direction, span_stiff, chord_stiff, span_live, chord_live, ground)
        step_size = precond_norm / inner_pq(direction, image)
        solution = solution + step_size[:, None, None, None] * direction
        residual = residual - step_size[:, None, None, None] * image
        if step + 1 < ITERS:
            precond = solve_blocks(factor, inverse, residual)
            norm_next = inner_rz(residual, precond)
            direction = precond + (norm_next / precond_norm)[:, None, None, None] * direction
            precond_norm = norm_next
    return (solution, residual)


def solution(mesh):
    return jax.shard_map(
        body,
        mesh=mesh,
        in_specs=(
            P(None, None, "slab", "sub"),
            P(None, "slab", "sub"),
            P(None, "slab", "sub"),
            P("slab", "sub"),
            P("slab", "sub"),
            P(None, "slab", "sub"),
            P(),
        ),
        out_specs=(P(None, None, "slab", "sub"), P(None, None, "slab", "sub")),
        check_vma=False,
    )
```

profile of v0, /device:TPU:1, one launch (start us, length us, event | category | flops | bytes accessed | tf_op | source)
XLA Modules:
  0.0 413.0 jit_solution(10485907390977975643)
XLA Ops:
  1.4 4.9 %collective-permute-start.4 = (f32[6,1,128]{2,1,0:T(1,128)S(1)}, f32[6,1,128]{2,1,0:T(1,128)S(1)}, u32[]{:S(2)}, u32[]{:S(2)}) collective-permute-start(f32[6,1,128]{2,1,0:T(1,128)S(1)} %slice.527), channel_id=1, source_target_pairs={{0,4},{4,8},{8,12},{12,16},{16,20},{20,24},{24,28},{28,32},{32,36}... | collective-permute-start | bytes 9224 | tf_op jit(solution)/shard_map/ppermute | solution.py:12
  7.1 3.1 collective-permute-start.5
  13.0 3.3 collective-permute-start
  27.8 2.2 collective-permute-start.1
  30.8 4.0 collective-permute-start.3
  40.5 3.8 collective-permute-start.6
  46.7 1.6 fusion.9
  49.1 2.1 collective-permute-start.8
  52.5 2.1 copy.16
  54.6 4.4 %collective-permute-start.9 = (f32[32,6,8,1]{0,2,3,1:T(8,128)}, f32[32,6,8,1]{0,2,3,1:T(8,128)}, u32[]{:S(2)}, u32[]{:S(2)}) collective-permute-start(f32[32,6,8,1]{0,2,3,1:T(8,128)} %copy.16), channel_id=1, source_target_pairs={{0,1},{1,2},{2,3},{4,5},{5,6},{6,7},{8,9},{9,10},{10,11},{12,13},{... | collective-permute-start | bytes 18440 | tf_op jit(solution)/shard_map/ppermute | solution.py:12
  59.5 2.0 copy.17
  61.5 2.6 multiply_reduce_fusion.2
  64.1 112.9 %all-reduce = (f32[32]{0:T(128)S(1)}, f32[32]{0:T(128)S(1)}) all-reduce(f32[32]{0:T(128)S(1)} %get-tuple-element.7, f32[32]{0:T(128)S(1)} %get-tuple-element.6), channel_id=1, replica_groups=mesh['slab'=128,'sub'=4] {'slab','sub'}, use_global_device_ids=true, to_apply=%region_3.0 | all-reduce | flops 64 | bytes 512 | tf_op jit(solution)/shard_map/psum | solution.py:82
  180.0 98.7 %psum.30 = f32[32]{0:T(128)S(1)} all-reduce(f32[32]{0:T(128)S(1)} %multiply_reduce_fusion.1), channel_id=1, replica_groups=mesh['slab'=128,'sub'=4] {'slab','sub'}, use_global_device_ids=true, to_apply=%region_9.0 | all-reduce | flops 32 | bytes 256 | tf_op jit(solution)/shard_map/psum | solution.py:82
  278.9 2.6 collective-permute-start.10
  284.3 2.3 collective-permute-done.11
  287.9 1.8 fusion.14
  291.4 4.5 %collective-permute-start.12 = (f32[32,6,1,128]{3,0,2,1:T(8,128)}, f32[32,6,1,128]{3,0,2,1:T(8,128)}, u32[]{:S(2)}, u32[]{:S(2)}) collective-permute-start(f32[32,6,1,128]{3,0,2,1:T(8,128)} %slice.798), channel_id=1, source_target_pairs={{0,4},{4,8},{8,12},{12,16},{16,20},{20,24},{24,28},{28,32},{32,36}... | collective-permute-start | bytes 294920 | tf_op jit(solution)/shard_map/ppermute | solution.py:12
  297.1 1.5 copy.20
  298.6 2.9 collective-permute-start.13
  301.5 2.0 slice.799
  304.7 2.7 multiply_reduce_fusion
  307.5 100.6 %psum.31 = f32[32]{0:T(128)S(1)} all-reduce(f32[32]{0:T(128)S(1)} %get-tuple-element.14), channel_id=1, replica_groups=mesh['slab'=128,'sub'=4] {'slab','sub'}, use_global_device_ids=true, to_apply=%region_13.0 | all-reduce | flops 32 | bytes 256 | tf_op jit(solution)/shard_map/psum | solution.py:86
  408.8 1.5 multiply_subtract_fusion
  (167 shorter events, 41.6 us)
Async XLA Ops:
  1.4 20.2 %collective-permute-start.4 = (f32[6,1,128]{2,1,0:T(1,128)S(1)}, f32[6,1,128]{2,1,0:T(1,128)S(1)}, u32[]{:S(2)}, u32[]{:S(2)}) collective-permute-start(f32[6,1,128]{2,1,0:T(1,128)S(1)} %slice.527), channel_id=1, source_target_pairs={{0,4},{4,8},{8,12},{12,16},{16,20},{20,24},{24,28},{28,32},{32,36}... | collective-permute-start | bytes 9224 | tf_op jit(solution)/shard_map/ppermute | solution.py:12
  7.1 13.7 %collective-permute-start.5 = (f32[6,8,1]{2,1,0:T(8,128)S(1)}, f32[6,8,1]{2,1,0:T(8,128)S(1)}, u32[]{:S(2)}, u32[]{:S(2)}) collective-permute-start(f32[6,8,1]{2,1,0:T(8,128)S(1)} %slice.531), channel_id=1, source_target_pairs={{0,1},{1,2},{2,3},{4,5},{5,6},{6,7},{8,9},{9,10},{10,11},{12,13},{... | collective-permute-start | bytes 584 | tf_op jit(solution)/shard_map/ppermute | solution.py:12
  11.7 14.3 %collective-permute-start.2 = (f32[32,6,8,1]{0,2,3,1:T(8,128)S(1)}, f32[32,6,8,1]{0,2,3,1:T(8,128)S(1)}, u32[]{:S(2)}, u32[]{:S(2)}) collective-permute-start(f32[32,6,8,1]{0,2,3,1:T(8,128)S(1)} %copy.10), channel_id=1, source_target_pairs={{1,0},{2,1},{3,2},{5,4},{6,5},{7,6},{9,8},{10,9},{11,10},{13,12},{... | collective-permute-start | bytes 18440 | tf_op jit(solution)/shard_map/ppermute | solution.py:12
  13.0 13.4 %collective-permute-start = (f32[32,6,1,128]{3,0,2,1:T(8,128)S(1)}, f32[32,6,1,128]{3,0,2,1:T(8,128)S(1)}, u32[]{:S(2)}, u32[]{:S(2)}) collective-permute-start(f32[32,6,1,128]{3,0,2,1:T(8,128)S(1)} %slice.661), channel_id=1, source_target_pairs={{4,0},{8,4},{12,8},{16,12},{20,16},{24,20},{28,24},{32,28},{36,32}... | collective-permute-start | bytes 294920 | tf_op jit(solution)/shard_map/ppermute | solution.py:12
  21.6 3.2 copy-start.7
  27.8 7.1 %copy-start = (f32[32,6,8,128]{3,0,2,1:T(8,128)}, f32[32,6,8,128]{3,0,2,1:T(8,128)S(1)}, u32[]{:S(2)}) copy-start(f32[32,6,8,128]{3,0,2,1:T(8,128)S(1)} %broadcast_multiply_fusion.5) | copy-start | bytes 2359300
  27.8 2.3 copy-start.21
  27.8 8.3 %collective-permute-start.1 = (f32[32,6,1,128]{3,0,2,1:T(8,128)S(1)}, f32[32,6,1,128]{3,0,2,1:T(8,128)}, u32[]{:S(2)}, u32[]{:S(2)}) collective-permute-start(f32[32,6,1,128]{3,0,2,1:T(8,128)S(1)} %slice.663), channel_id=1, source_target_pairs={{0,4},{4,8},{8,12},{12,16},{16,20},{20,24},{24,28},{28,32},{32,36}... | collective-permute-start | bytes 294920 | tf_op jit(solution)/shard_map/ppermute | solution.py:12
  30.5 4.4 %copy-start.8 = (f32[8,129]{1,0:T(8,128)S(1)}, f32[8,129]{1,0:T(8,128)}, u32[]{:S(2)}) copy-start(f32[8,129]{1,0:T(8,128)} %copy-done.7) | copy-start | bytes 12388
  30.5 4.4 %copy-start.20 = (f32[8,128]{1,0:T(8,128)S(1)}, f32[8,128]{1,0:T(8,128)}, u32[]{:S(2)}) copy-start(f32[8,128]{1,0:T(8,128)} %copy-done.19) | copy-start | bytes 12292
  30.8 4.9 %collective-permute-start.3 = (f32[32,6,8,1]{0,2,3,1:T(8,128)S(1)}, f32[32,6,8,1]{0,2,3,1:T(8,128)S(1)}, u32[]{:S(2)}, u32[]{:S(2)}) collective-permute-start(f32[32,6,8,1]{0,2,3,1:T(8,128)S(1)} %copy.12), channel_id=1, source_target_pairs={{0,1},{1,2},{2,3},{4,5},{5,6},{6,7},{8,9},{9,10},{10,11},{12,13},{... | collective-permute-start | bytes 18440 | tf_op jit(solution)/shard_map/ppermute | solution.py:12
  38.8 5.5 %copy-start.24 = (pred[9,128]{1,0:T(8,128)(4,1)S(1)}, pred[9,128]{1,0:T(8,128)(4,1)}, u32[]{:S(2)}) copy-start(pred[9,128]{1,0:T(8,128)(4,1)} %copy-done.23) | copy-start | bytes 3460
  39.2 6.4 %collective-permute-start.7 = (f32[32,6,8,1]{0,2,3,1:T(8,128)S(1)}, f32[32,6,8,1]{0,2,3,1:T(8,128)S(1)}, u32[]{:S(2)}, u32[]{:S(2)}) collective-permute-start(f32[32,6,8,1]{0,2,3,1:T(8,128)S(1)} %copy.14), channel_id=1, source_target_pairs={{1,0},{2,1},{3,2},{5,4},{6,5},{7,6},{9,8},{10,9},{11,10},{13,12},{... | collective-permute-start | bytes 18440 | tf_op jit(solution)/shard_map/ppermute | solution.py:12
  40.5 6.2 %collective-permute-start.6 = (f32[32,6,1,128]{3,0,2,1:T(8,128)S(1)}, f32[32,6,1,128]{3,0,2,1:T(8,128)S(1)}, u32[]{:S(2)}, u32[]{:S(2)}) collective-permute-start(f32[32,6,1,128]{3,0,2,1:T(8,128)S(1)} %slice.781), channel_id=1, source_target_pairs={{4,0},{8,4},{12,8},{16,12},{20,16},{24,20},{28,24},{32,28},{36,32}... | collective-permute-start | bytes 294920 | tf_op jit(solution)/shard_map/ppermute | solution.py:12
  44.4 3.9 copy-start.17
  48.4 10.6 %copy-start.1 = (f32[32,6,8,128]{3,0,2,1:T(8,128)}, f32[32,6,8,128]{3,0,2,1:T(8,128)S(1)}, u32[]{:S(2)}) copy-start(f32[32,6,8,128]{3,0,2,1:T(8,128)S(1)} %broadcast_multiply_fusion.3) | copy-start | bytes 2359300
  48.4 2.8 copy-start.9
  49.1 12.4 %collective-permute-start.8 = (f32[32,6,1,128]{3,0,2,1:T(8,128)}, f32[32,6,1,128]{3,0,2,1:T(8,128)}, u32[]{:S(2)}, u32[]{:S(2)}) collective-permute-start(f32[32,6,1,128]{3,0,2,1:T(8,128)} %slice.784), channel_id=1, source_target_pairs={{0,4},{4,8},{8,12},{12,16},{16,20},{20,24},{24,28},{28,32},{32,36}... | collective-permute-start | bytes 294920 | tf_op jit(solution)/shard_map/ppermute | solution.py:12
  54.6 4.9 %collective-permute-start.9 = (f32[32,6,8,1]{0,2,3,1:T(8,128)}, f32[32,6,8,1]{0,2,3,1:T(8,128)}, u32[]{:S(2)}, u32[]{:S(2)}) collective-permute-start(f32[32,6,8,1]{0,2,3,1:T(8,128)} %copy.16), channel_id=1, source_target_pairs={{0,1},{1,2},{2,3},{4,5},{5,6},{6,7},{8,9},{9,10},{10,11},{12,13},{... | collective-permute-start | bytes 18440 | tf_op jit(solution)/shard_map/ppermute | solution.py:12
  59.0 2.5 slice-start.1
  278.9 9.0 %collective-permute-start.10 = (f32[32,6,1,128]{3,0,2,1:T(8,128)S(1)}, f32[32,6,1,128]{3,0,2,1:T(8,128)S(1)}, u32[]{:S(2)}, u32[]{:S(2)}) collective-permute-start(f32[32,6,1,128]{3,0,2,1:T(8,128)S(1)} %slice.795), channel_id=1, source_target_pairs={{4,0},{8,4},{12,8},{16,12},{20,16},{24,20},{28,24},{32,28},{36,32}... | collective-permute-start | bytes 294920 | tf_op jit(solution)/shard_map/ppermute | solution.py:12
  281.8 4.8 %collective-permute-start.11 = (f32[32,6,8,1]{0,2,3,1:T(8,128)S(1)}, f32[32,6,8,1]{0,2,3,1:T(8,128)S(1)}, u32[]{:S(2)}, u32[]{:S(2)}) collective-permute-start(f32[32,6,8,1]{0,2,3,1:T(8,128)S(1)} %copy.18), channel_id=1, source_target_pairs={{1,0},{2,1},{3,2},{5,4},{6,5},{7,6},{9,8},{10,9},{11,10},{13,12},{... | collective-permute-start | bytes 18440 | tf_op jit(solution)/shard_map/ppermute | solution.py:12
  291.4 13.3 %collective-permute-start.12 = (f32[32,6,1,128]{3,0,2,1:T(8,128)}, f32[32,6,1,128]{3,0,2,1:T(8,128)}, u32[]{:S(2)}, u32[]{:S(2)}) collective-permute-start(f32[32,6,1,128]{3,0,2,1:T(8,128)} %slice.798), channel_id=1, source_target_pairs={{0,4},{4,8},{8,12},{12,16},{16,20},{20,24},{24,28},{28,32},{32,36}... | collective-permute-start | bytes 294920 | tf_op jit(solution)/shard_map/ppermute | solution.py:12
  298.6 4.9 %collective-permute-start.13 = (f32[32,6,8,1]{0,2,3,1:T(8,128)S(1)}, f32[32,6,8,1]{0,2,3,1:T(8,128)S(1)}, u32[]{:S(2)}, u32[]{:S(2)}) collective-permute-start(f32[32,6,8,1]{0,2,3,1:T(8,128)S(1)} %copy.20), channel_id=1, source_target_pairs={{0,1},{1,2},{2,3},{4,5},{5,6},{6,7},{8,9},{9,10},{10,11},{12,13},{... | collective-permute-start | bytes 18440 | tf_op jit(solution)/shard_map/ppermute | solution.py:12
  (22 other events, 19.8 us)
where the time goes:
time: 415 us; the launch traced here: 413 us
  blocking collectives  312 us (75%)
  starting transfers between devices  41.7 us (10%)
  local copies, waits for them, and re-layouts  31.7 us (8%)
  other arithmetic  21.5 us (5%)
  waiting for transfers between devices  4.56 us (1%)
    psum x2, blocking collectives, inner_rz(): return lax.psum(jnp.sum(first * second, axis=(1, 2, 3)), ('slab', 'sub'))  212 us
    psum x1, blocking collectives, inner_pq(): return lax.psum(jnp.sum(first * second, axis=(1, 2, 3)), ('slab', 'sub'))  101 us
    ppermute x14, starting transfers between devices, from_behind(): lax.ppermute(value, axis, [(source, source + steps) for source in range(i...  41.7 us
    unnamed x64, local copies, waits for them, and re-layouts  10.6 us
  transfers between devices with their start and end apart: 14, of which 4 were waited for; matrix products, arithmetic and copies ran while one was open for 6% of the time, Pallas kernels for 0%

commit v1 on v0

--- a/solution.py
+++ b/solution.py
@@ -1,9 +1,20 @@
+import functools
 import jax
 import jax.numpy as jnp
 from jax import lax
 from jax.sharding import PartitionSpec as P
+from jax.lax import psum
 
 ITERS = 2
+
+
+def post_samples_all(local_values, device_axis, mesh_dim):
+    for src_i in (device_axis, mesh_dim):
+        local_values = psum(local_values, axis_name=src_i)
+    return local_values
+
+
+open_the_pools = functools.partial(post_samples_all, device_axis="slab", mesh_dim="sub")
 
 
 def from_behind(value, axis, steps):
@@ -83,7 +94,7 @@
 
 
 def inner_pq(first, second):
-    return lax.psum(jnp.sum(first * second, axis=(1, 2, 3)), ("slab", "sub"))
+    return open_the_pools(jnp.sum(first * second, axis=(1, 2, 3)))
 
 
 def body(mode_shapes, span_stiff, chord_stiff, span_geo, chord_geo, ground, chord_len):

time: 415 us -> 820 us (1.98)
  blocking collectives: 312 us -> 717 us
    psum x1 -> x4, blocking collectives: 101 us -> 516 us  [post_samples_all(): local_values = psum(local_values, axis_name=src_i)]
    psum x2, blocking collectives: 212 us -> 202 us  [inner_rz(): return lax.psum(jnp.sum(first * second, axis=(1, 2, 3)), ('slab', 'sub'))]
  transfers between devices with their start and end apart: 14 -> 14, of which waited for: 4 -> 4; matrix products, arithmetic and copies ran while one was open for 6% -> 3% of each run, Pallas kernels for 0% -> 0%
where the time goes in v1:
time: 820 us; the launch traced here: 818 us
  blocking collectives  717 us (87%)
  starting transfers between devices  41.3 us (5%)
  local copies, waits for them, and re-layouts  31.6 us (4%)
  other arithmetic  21.5 us (3%)
    psum x4, blocking collectives, post_samples_all(): local_values = psum(local_values, axis_name=src_i)  516 us
    psum x2, blocking collectives, inner_rz(): return lax.psum(jnp.sum(first * second, axis=(1, 2, 3)), ('slab', 'sub'))  202 us
    ppermute x14, starting transfers between devices, from_behind(): lax.ppermute(value, axis, [(source, source + steps) for source in range(i...  41.3 us
  transfers between devices with their start and end apart: 14, of which 4 were waited for; matrix products, arithmetic and copies ran while one was open for 3% of the time, Pallas kernels for 0%

profile of v1, /device:TPU:1, one launch (start us, length us, event | category | flops | bytes accessed | tf_op | source)
XLA Modules:
  0.0 817.7 jit_solution(14137330776508560358)
XLA Ops:
  1.4 4.9 collective-permute-start.4
  7.1 3.1 collective-permute-start.5
  13.0 3.3 collective-permute-start
  27.8 2.2 collective-permute-start.1
  30.8 4.0 collective-permute-start.3
  40.5 3.8 collective-permute-start.6
  49.1 2.1 collective-permute-start.8
  52.5 2.1 copy.16
  54.6 4.4 collective-permute-start.9
  59.5 2.0 copy.17
  61.5 2.6 multiply_reduce_fusion.2
  64.1 252.7 %psum.43 = f32[32]{0:T(128)S(1)} all-reduce(f32[32]{0:T(128)S(1)} %get-tuple-element.6), channel_id=1, replica_groups=mesh['slab'=128,'sub'=4] {'slab'}, use_global_device_ids=true, to_apply=%region_7.0 | all-reduce | flops 32 | bytes 256 | tf_op jit(solution)/shard_map/psum | solution.py:13
  316.8 10.0 %psum.44 = f32[32]{0:T(128)S(1)} all-reduce(f32[32]{0:T(128)S(1)} %psum.43), channel_id=1, replica_groups=mesh['slab'=128,'sub'=4] {'sub'}, use_global_device_ids=true, to_apply=%region_8.0 | all-reduce | flops 32 | bytes 256 | tf_op jit(solution)/shard_map/psum | solution.py:13
  326.8 101.1 %psum.42 = f32[32]{0:T(128)S(1)} all-reduce(f32[32]{0:T(128)S(1)} %get-tuple-element.7), channel_id=1, replica_groups=mesh['slab'=128,'sub'=4] {'slab','sub'}, use_global_device_ids=true, to_apply=%region_3.0 | all-reduce | flops 32 | bytes 256 | tf_op jit(solution)/shard_map/psum | solution.py:93
  430.8 100.5 %psum.45 = f32[32]{0:T(128)S(1)} all-reduce(f32[32]{0:T(128)S(1)} %multiply_reduce_fusion.1), channel_id=1, replica_groups=mesh['slab'=128,'sub'=4] {'slab','sub'}, use_global_device_ids=true, to_apply=%region_10.0 | all-reduce | flops 32 | bytes 256 | tf_op jit(solution)/shard_map/psum | solution.py:93
  531.6 2.6 collective-permute-start.10
  537.0 2.3 collective-permute-done.11
  540.6 1.8 fusion.14
  544.1 3.9 collective-permute-start.12
  550.7 3.0 collective-permute-start.13
  553.7 2.0 slice.799
  557.0 2.7 multiply_reduce_fusion
  559.8 245.6 %psum.46 = f32[32]{0:T(128)S(1)} all-reduce(f32[32]{0:T(128)S(1)} %get-tuple-element.12), channel_id=1, replica_groups=mesh['slab'=128,'sub'=4] {'slab'}, use_global_device_ids=true, to_apply=%region_14.0 | all-reduce | flops 32 | bytes 256 | tf_op jit(solution)/shard_map/psum | solution.py:13
  805.4 7.5 psum.47
  (170 shorter events, 46.0 us)
Async XLA Ops:
  1.4 20.2 %collective-permute-start.4 = (f32[6,1,128]{2,1,0:T(1,128)S(1)}, f32[6,1,128]{2,1,0:T(1,128)S(1)}, u32[]{:S(2)}, u32[]{:S(2)}) collective-permute-start(f32[6,1,128]{2,1,0:T(1,128)S(1)} %slice.527), channel_id=1, source_target_pairs={{0,4},{4,8},{8,12},{12,16},{16,20},{20,24},{24,28},{28,32},{32,36}... | collective-permute-start | bytes 9224 | tf_op jit(solution)/shard_map/ppermute | solution.py:23
  7.1 13.7 %collective-permute-start.5 = (f32[6,8,1]{2,1,0:T(8,128)S(1)}, f32[6,8,1]{2,1,0:T(8,128)S(1)}, u32[]{:S(2)}, u32[]{:S(2)}) collective-permute-start(f32[6,8,1]{2,1,0:T(8,128)S(1)} %slice.531), channel_id=1, source_target_pairs={{0,1},{1,2},{2,3},{4,5},{5,6},{6,7},{8,9},{9,10},{10,11},{12,13},{... | collective-permute-start | bytes 584 | tf_op jit(solution)/shard_map/ppermute | solution.py:23
  11.7 14.3 %collective-permute-start.2 = (f32[32,6,8,1]{0,2,3,1:T(8,128)S(1)}, f32[32,6,8,1]{0,2,3,1:T(8,128)S(1)}, u32[]{:S(2)}, u32[]{:S(2)}) collective-permute-start(f32[32,6,8,1]{0,2,3,1:T(8,128)S(1)} %copy.10), channel_id=1, source_target_pairs={{1,0},{2,1},{3,2},{5,4},{6,5},{7,6},{9,8},{10,9},{11,10},{13,12},{... | collective-permute-start | bytes 18440 | tf_op jit(solution)/shard_map/ppermute | solution.py:23
  13.0 13.3 %collective-permute-start = (f32[32,6,1,128]{3,0,2,1:T(8,128)S(1)}, f32[32,6,1,128]{3,0,2,1:T(8,128)S(1)}, u32[]{:S(2)}, u32[]{:S(2)}) collective-permute-start(f32[32,6,1,128]{3,0,2,1:T(8,128)S(1)} %slice.661), channel_id=1, source_target_pairs={{4,0},{8,4},{12,8},{16,12},{20,16},{24,20},{28,24},{32,28},{36,32}... | collective-permute-start | bytes 294920 | tf_op jit(solution)/shard_map/ppermute | solution.py:23
  21.6 3.2 copy-start.7
  27.8 7.1 copy-start
  27.8 2.3 copy-start.21
  27.8 8.3 %collective-permute-start.1 = (f32[32,6,1,128]{3,0,2,1:T(8,128)S(1)}, f32[32,6,1,128]{3,0,2,1:T(8,128)}, u32[]{:S(2)}, u32[]{:S(2)}) collective-permute-start(f32[32,6,1,128]{3,0,2,1:T(8,128)S(1)} %slice.663), channel_id=1, source_target_pairs={{0,4},{4,8},{8,12},{12,16},{16,20},{20,24},{24,28},{28,32},{32,36}... | collective-permute-start | bytes 294920 | tf_op jit(solution)/shard_map/ppermute | solution.py:23
  30.5 4.4 copy-start.8
  30.5 4.4 copy-start.20
  30.8 4.9 collective-permute-start.3
  38.8 5.5 copy-start.24
  39.2 6.4 collective-permute-start.7
  40.5 6.2 collective-permute-start.6
  44.3 3.9 copy-start.17
  48.4 10.6 %copy-start.1 = (f32[32,6,8,128]{3,0,2,1:T(8,128)}, f32[32,6,8,128]{3,0,2,1:T(8,128)S(1)}, u32[]{:S(2)}) copy-start(f32[32,6,8,128]{3,0,2,1:T(8,128)S(1)} %broadcast_multiply_fusion.3) | copy-start | bytes 2359300
  48.4 2.8 copy-start.9
  49.1 12.4 %collective-permute-start.8 = (f32[32,6,1,128]{3,0,2,1:T(8,128)}, f32[32,6,1,128]{3,0,2,1:T(8,128)}, u32[]{:S(2)}, u32[]{:S(2)}) collective-permute-start(f32[32,6,1,128]{3,0,2,1:T(8,128)} %slice.784), channel_id=1, source_target_pairs={{0,4},{4,8},{8,12},{12,16},{16,20},{20,24},{24,28},{28,32},{32,36}... | collective-permute-start | bytes 294920 | tf_op jit(solution)/shard_map/ppermute | solution.py:23
  54.6 4.9 collective-permute-start.9
  59.0 2.5 slice-start.1
  531.6 9.0 %collective-permute-start.10 = (f32[32,6,1,128]{3,0,2,1:T(8,128)S(1)}, f32[32,6,1,128]{3,0,2,1:T(8,128)S(1)}, u32[]{:S(2)}, u32[]{:S(2)}) collective-permute-start(f32[32,6,1,128]{3,0,2,1:T(8,128)S(1)} %slice.795), channel_id=1, source_target_pairs={{4,0},{8,4},{12,8},{16,12},{20,16},{24,20},{28,24},{32,28},{36,32}... | collective-permute-start | bytes 294920 | tf_op jit(solution)/shard_map/ppermute | solution.py:23
  534.5 4.8 collective-permute-start.11
  544.1 12.9 %collective-permute-start.12 = (f32[32,6,1,128]{3,0,2,1:T(8,128)}, f32[32,6,1,128]{3,0,2,1:T(8,128)}, u32[]{:S(2)}, u32[]{:S(2)}) collective-permute-start(f32[32,6,1,128]{3,0,2,1:T(8,128)} %slice.798), channel_id=1, source_target_pairs={{0,4},{4,8},{8,12},{12,16},{16,20},{20,24},{24,28},{28,32},{32,36}... | collective-permute-start | bytes 294920 | tf_op jit(solution)/shard_map/ppermute | solution.py:23
  550.7 5.1 collective-permute-start.13
  (22 other events, 19.7 us)
